TPU v7x, 512 devices: a whole 4x8x8 slice. The times are simulated.
512 devices in a mesh: row: 16 (over y_lo, x, core), col: 32 (over z, y_hi).
Axes of the slice: x: 4, y: 8 (y_hi: 4, y_lo: 2; y = y_hi * 2 + y_lo), z: 8, core: 2. Of those that a mesh axis runs over, the one named last changes fastest.
Arguments:
- act_values: bfloat16 [2048, 16384], P('col', 'row'), may hold values from -6 to 6
- act_scales: float32 [2048, 128], P('col', 'row'), may hold values from 0.3 to 4
- grad_values: bfloat16 [2048, 28672], P('row', 'col'), may hold values from -6 to 6
- grad_scales: float32 [2048, 224], P('row', 'col'), may hold values from 0.3 to 4
- weight: bfloat16 [16384, 28672], P('row', 'col'), may hold values from -0.03125 to 0.03125
Outputs:
- input_grad: bfloat16 [2048, 16384], P('col', 'row')
- weight_grad: bfloat16 [16384, 28672], P('row', 'col')
All inputs are finite; a program needn't handle non-finite values.
Results may differ from a plain program's by a relative error of at most 0.015.
Values may be sent and summed in bfloat16 or wider, within the bound.
No kernel may reach another device: no remote copies, remote signals or barrier semaphores. Data moves between devices by JAX's collectives and lax.ppermute only.
A program may use at most 64 MiB of HBM per device.

v0:
```python
import jax
import jax.numpy as jnp
from jax import lax
from jax.sharding import PartitionSpec as P

QB = 128


def dequantize(values, scales):
    height, breadth = values.shape
    scaled = values.astype(jnp.float32).reshape(height, breadth // QB, QB) * scales[:, :, None]
    return scaled.reshape(height, breadth).astype(jnp.bfloat16)


def shards(act_values, act_scales, grad_values, grad_scales, weight):
    act_local = dequantize(act_values, act_scales)
    grad_local = dequantize(grad_values, grad_scales)
    activations = lax.all_gather(act_local, "col", axis=0, tiled=True)
    gradients = lax.all_gather(grad_local, "row", axis=0, tiled=True)
    weight_grad = lax.dot_general(
        activations, gradients, (((0,), (0,)), ((), ())), preferred_element_type=jnp.float32
    ).astype(jnp.bfloat16)
    summed = lax.psum_scatter(
        lax.dot_general(
            gradients, weight, (((1,), (1,)), ((), ())), preferred_element_type=jnp.float32
        ).astype(jnp.bfloat16),
        "col",
        scatter_dimension=0,
        tiled=True,
    )
    return (summed, weight_grad)


def solution(mesh):
    placed = (P("col", "row"), P("col", "row"), P("row", "col"), P("row", "col"), P("row", "col"))
    return jax.shard_map(
        shards,
        mesh=mesh,
        in_specs=placed,
        out_specs=(P("col", "row"), P("row", "col")),
        check_vma=False,
    )
```

profile of v0, /device:TPU:2, one launch (start us, length us, event | category | flops | bytes accessed | tf_op | source)
XLA Modules:
  0.0 411.5 jit_solution(16351301246919904140)
XLA Ops:
  7.2 0.0 copy-start
  7.2 0.0 all-gather.3.cloned.1.call-start
  7.2 1.2 copy.9
  8.5 1.4 fusion
  9.9 0.0 all-gather.3.cloned.1.call-update
  9.9 0.0 all-gather.5.cloned.1.call-start
  10.0 0.8 copy.10
  10.7 0.1 mul.25
  10.9 1.6 fusion.1
  12.5 0.0 all-gather.5.cloned.1.call-update
  12.5 0.0 reduce-scatter.2.cloned.1.call-start
  12.5 50.8 %all-gather.3.cloned.1.call-done = bf16[2048,896]{0,1:T(8,128)(2,1)} async-done(((bf16[128,896]{0,1:T(8,128)(2,1)}), bf16[2048,896]{0,1:T(8,128)(2,1)}) %all-gather.3.cloned.1.call-update) | async-done | bytes 3670032 | tf_op jit(solution)/shard_map/all_gather | solution.py:19
  63.3 0.0 copy-done
  63.3 8.3 %convolution_convert_fusion = bf16[2048,1024]{1,0:T(8,128)(2,1)} fusion(bf16[2048,896]{0,1:T(8,128)(2,1)} %all-gather.3.cloned.1.call-done, bf16[1024,896]{1,0:T(8,128)(2,1)S(1)} %copy-done), kind=kOutput, calls=%fused_computation | convolution fusion | flops 3760193536 | bytes 9699328 | tf_op jit(solution)/shard_map/dot_general | solution.py:24
  71.6 0.0 reduce-scatter.2.cloned.1.call-update
  71.6 98.3 %all-gather.5.cloned.1.call-done = bf16[2048,1024]{1,0:T(8,128)(2,1)} async-done(((bf16[64,1024]{1,0:T(8,128)(2,1)}), bf16[2048,1024]{1,0:T(8,128)(2,1)}) %all-gather.5.cloned.1.call-update) | async-done | bytes 4194320 | tf_op jit(solution)/shard_map/all_gather | solution.py:18
  169.9 9.1 %convolution_convert_fusion.1 = bf16[1024,896]{1,0:T(8,128)(2,1)} fusion(bf16[2048,1024]{1,0:T(8,128)(2,1)} %all-gather.5.cloned.1.call-done, bf16[2048,896]{0,1:T(8,128)(2,1)} %all-gather.3.cloned.1.call-done), kind=kOutput, calls=%fused_computation.1 | convolution fusion | flops 3759013888 | bytes 9699328 | tf_op jit(solution)/shard_map/dot_general | solution.py:20
  179.0 226.0 %reduce-scatter.2.cloned.1.call-done = bf16[64,1024]{1,0:T(8,128)(2,1)} async-done(((bf16[2048,1024]{1,0:T(8,128)(2,1)}), bf16[64,1024]{1,0:T(8,128)(2,1)}) %reduce-scatter.2.cloned.1.call-update) | async-done | bytes 131088 | tf_op jit(solution)/shard_map/reduce_scatter | solution.py:23
Async XLA Ops:
  7.2 56.2 %copy-start = (bf16[1024,896]{1,0:T(8,128)(2,1)S(1)}, bf16[1024,896]{1,0:T(8,128)(2,1)}, u32[]{:S(2)}) copy-start(bf16[1024,896]{1,0:T(8,128)(2,1)} %param.9) | copy-start | bytes 5505028
  7.2 56.2 %all-gather.3.cloned.1.call-start = ((), (), s32[]{:S(2)}) async-start(), calls=%async_computation.1 | async-start | bytes 3899392 | tf_op jit(solution)/shard_map/all_gather | solution.py:19
  9.9 160.0 %all-gather.5.cloned.1.call-start = ((), (), s32[]{:S(2)}) async-start(), calls=%async_computation.3 | async-start | bytes 4325376 | tf_op jit(solution)/shard_map/all_gather | solution.py:18
  12.5 392.5 %reduce-scatter.2.cloned.1.call-start = ((), (), s32[]{:S(2)}) async-start(), calls=%async_computation.2 | async-start | bytes 4325376 | tf_op jit(solution)/shard_map/reduce_scatter | solution.py:23
Sparse Core Ops, SparseCore 0:
  10.6 52.6 all-gather.2
  66.5 103.3 all-gather.4
  175.0 229.9 reduce-scatter.1
where the time goes:
time: 412 us
  waiting for transfers between devices  375 us (91%)
  matrix products  17.4 us (4%)
  between operations  13.8 us (3%)
    reduce_scatter x1, waiting for transfers between devices, shards(): lax.psum_scatter(lax.dot_general(gradients, weight, (((1,), (1,)), ((), (...  226 us
    all_gather x1, waiting for transfers between devices, shards(): activations = lax.all_gather(act_local, 'col', axis=0, tiled=True)  98.3 us
    all_gather x1, waiting for transfers between devices, shards(): gradients = lax.all_gather(grad_local, 'row', axis=0, tiled=True)  50.8 us
    dot_general x1, matrix products, shards(): lax.dot_general(activations, gradients, (((0,), (0,)), ((), ())), preferr...  9.09 us
    dot_general x1, matrix products, shards(): lax.dot_general(gradients, weight, (((1,), (1,)), ((), ())), preferred_el...  8.28 us
  transfers between devices with their start and end apart: 3, of which 3 were waited for; matrix products, arithmetic and copies ran while one was open for 5% of the time, Pallas kernels for 0%

commit v1 on v0

v1 whole, which is shorter than its diff:
```python
import jax
import jax.numpy as jnp
from jax import lax
from jax.experimental import pallas as pl
from jax.experimental.pallas import tpu as pltpu
from jax.sharding import Mesh, PartitionSpec as P


QB = 128
NY = 4
NZ = 8
ROW = ("ylo", "x", "core")
COL = ("z", "yhi")


def dequantize(values, scales):
    height, breadth = values.shape
    scaled = values.astype(jnp.float32).reshape(height, breadth // QB, QB) * scales[:, :, None]
    return scaled.reshape(height, breadth).astype(jnp.bfloat16)


def shift(array, axis, size, by):
    return lax.ppermute(array, axis, [(i, (i + by) % size) for i in range(size)])


def partial_kernel(grad_ref, weight_ref, out_ref):
    out_ref[...] = lax.dot_general(
        grad_ref[...], weight_ref[...], (((1,), (1,)), ((), ())), preferred_element_type=jnp.float32
    ).astype(out_ref.dtype)


def partial_product(gradients, weight, tile=256):
    tokens, hidden = gradients.shape
    width = weight.shape[0]
    return pl.pallas_call(
        partial_kernel,
        grid=(tokens // tile,),
        in_specs=[
            pl.BlockSpec((tile, hidden), lambda i: (i, 0)),
            pl.BlockSpec((width, hidden), lambda i: (0, 0)),
        ],
        out_specs=pl.BlockSpec((tile, width), lambda i: (i, 0)),
        out_shape=jax.ShapeDtypeStruct((tokens, width), jnp.bfloat16),
        cost_estimate=pl.CostEstimate(
            flops=2 * tokens * hidden * width,
            bytes_accessed=2 * (tokens * hidden + hidden * width + tokens * width),
            transcendentals=0,
        ),
        name="partial_product",
    )(gradients, weight)


def mark_kernel(*refs):
    refs[-1][...] = jnp.zeros_like(refs[-1])


def mark(*arrays):
    return pl.pallas_call(
        mark_kernel,
        in_specs=[pl.BlockSpec(memory_space=pl.ANY)] * len(arrays),
        out_shape=jax.ShapeDtypeStruct((8, 128), jnp.float32),
        cost_estimate=pl.CostEstimate(flops=0, bytes_accessed=4096, transcendentals=0),
        name="mark",
    )(*arrays)


def outer_kernel(places, z_ref, grad_ref, *refs):
    out_ref = refs[-1]
    z = z_ref[0]
    total = None
    for (hop, first, rows), act_ref in zip(places, refs[:-1]):
        start = ((z + hop) & (NZ - 1)) * (grad_ref.shape[0] // NZ) + first
        grads = grad_ref[pl.ds(pl.multiple_of(start, rows), rows), :]
        term = lax.dot_general(
            act_ref[...], grads, (((0,), (0,)), ((), ())), preferred_element_type=jnp.float32
        )
        total = term if total is None else total + term
    out_ref[...] = total.astype(out_ref.dtype)


def outer_product(held, gradients, z, marks, tile=256):
    tokens, hidden = gradients.shape
    width = held[0][1].shape[1]
    places = tuple(place for place, _ in held)
    arrays = [array for _, array in held]

    def kernel(*refs):
        outer_kernel(places, *refs[: 2 + len(arrays)], refs[-1])

    return pl.pallas_call(
        kernel,
        grid=(width // tile,),
        in_specs=[
            pl.BlockSpec(memory_space=pltpu.SMEM),
            pl.BlockSpec((tokens, hidden), lambda i: (0, 0)),
        ]
        + [pl.BlockSpec((array.shape[0], tile), lambda i: (0, i)) for array in arrays]
        + [pl.BlockSpec(memory_space=pl.ANY)] * len(marks),
        out_specs=pl.BlockSpec((tile, hidden), lambda i: (i, 0)),
        out_shape=jax.ShapeDtypeStruct((width, hidden), jnp.bfloat16),
        cost_estimate=pl.CostEstimate(
            flops=2 * tokens * hidden * width,
            bytes_accessed=2 * (tokens * hidden + hidden * width + tokens * width),
            transcendentals=0,
        ),
        name="outer_product",
    )(jnp.full((1,), z, jnp.int32), gradients, *arrays, *marks)


def gather_over_yhi(local):
    y = lax.axis_index("yhi")
    rows, cols = local.shape
    pieces = [(0, local)]
    for k in (1, 3, 2):
        pieces.append((k, shift(local, "yhi", NY, k)))
    block = jnp.zeros((NY * rows, cols), local.dtype)
    for k, piece in pieces:
        block = lax.dynamic_update_slice(block, piece, (((y - k) & (NY - 1)) * rows, 0))
    return block


def ring_over_z(block):
    rows = block.shape[0]
    half = rows // 2
    held = [((0, 0, rows), block)]
    up, down = block, block
    marks = []
    for step in range(1, NZ // 2):
        up = shift(up, "z", NZ, 1)
        down = shift(down, "z", NZ, -1)
        held += [((-step, 0, rows), up), ((step, 0, rows), down)]
        if step in (1, 3):
            marks.append(mark(up, down))
    up = shift(up[:half], "z", NZ, 1)
    down = shift(down[half:], "z", NZ, -1)
    held += [((NZ // 2, 0, half), up), ((NZ // 2, half, half), down)]
    return held, marks


def shards(act_values, act_scales, grad_values, grad_scales, weight):
  grad_local = dequantize(grad_values, grad_scales)
  gradients = lax.all_gather(grad_local, ROW, axis=0, tiled=True)
  act_local = dequantize(act_values, act_scales)
  held, marks = ring_over_z(gather_over_yhi(act_local))
  partial = partial_product(gradients, weight)
  over_z = lax.psum_scatter(partial, "z", scatter_dimension=0, tiled=True)
  rows = act_local.shape[0]
  blocks = lax.all_to_all(over_z, "yhi", 0, 0, tiled=True).reshape(NY, rows, -1)
  summed = jnp.sum(blocks.astype(jnp.float32), axis=0).astype(jnp.bfloat16)
  weight_grad = outer_product(held, gradients, lax.axis_index("z"), marks)
  return (summed, weight_grad)


def solution(mesh):
    fine = Mesh(mesh.devices.reshape(2, 4, 2, NZ, NY), ROW + COL)
    placed = (P(COL, ROW), P(COL, ROW), P(ROW, COL), P(ROW, COL), P(ROW, COL))
    return jax.shard_map(
        shards,
        mesh=fine,
        in_specs=placed,
        out_specs=(P(COL, ROW), P(ROW, COL)),
        check_vma=False,
    )
```

time: 412 us -> 195 us (0.47)
  the two profiles are of different devices: /device:TPU:2 before, /device:TPU:8 now
where the time goes in v1:
time: 195 us; the launch traced here: 194 us
  waiting for transfers between devices  105 us (54%)
  starting transfers between devices  50 us (26%)
  Pallas kernels  20.3 us (10%)
  between operations  14.3 us (7%)
  local copies, waits for them, and re-layouts  2.68 us (1%)
  other arithmetic  2.48 us (1%)
    ppermute x11, waiting for transfers between devices, shift(): lax.ppermute(array, axis, [(i, (i + by) % size) for i in range(size)])  57.6 us
    all_gather x1, waiting for transfers between devices, shards(): gradients = lax.all_gather(grad_local, ROW, axis=0, tiled=True)  46.9 us
    ppermute x11, starting transfers between devices, shift(): lax.ppermute(array, axis, [(i, (i + by) % size) for i in range(size)])  44.1 us
    pallas_call x1, Pallas kernels, partial_product(): pl.pallas_call(partial_kernel, grid=(tokens // tile,), in_specs=[pl.Block...  9.92 us
    pallas_call x1, Pallas kernels, outer_product(): pl.pallas_call(kernel, grid=(width // tile,), in_specs=[pl.BlockSpec(memo...  9.2 us
    all_to_all x1, starting transfers between devices, shards(): lax.all_to_all(over_z, 'yhi', 0, 0, tiled=True).reshape(NY, rows, -1)  5.85 us
  transfers between devices with their start and end apart: 14, of which 7 were waited for; matrix products, arithmetic and copies ran while one was open for 1% of the time, Pallas kernels for 5%

profile of v1, /device:TPU:8, one launch (start us, length us, event | category | flops | bytes accessed | tf_op | source)
XLA Modules:
  0.0 194.4 jit_solution(15785538371278997771)
XLA Ops:
  7.2 0.7 mul.34
  7.9 0.2 copy.9
  8.1 1.7 multiply_convert_fusion
  9.9 46.9 %all-gather.2.cloned.1.call-done.grad_ref.refs_1_ = bf16[2048,896]{1,0:T(8,128)(2,1)} async-done(((bf16[128,896]{1,0:T(8,128)(2,1)}), bf16[2048,896]{1,0:T(8,128)(2,1)}) %all-gather.2.cloned.1.call-update) | async-done | bytes 3670032 | tf_op jit(solution)/shard_map/all_gather | solution.py:142
  56.8 9.9 %partial_product.1 = bf16[2048,1024]{1,0:T(8,128)(2,1)} custom-call(bf16[2048,896]{1,0:T(8,128)(2,1)} %all-gather.2.cloned.1.call-done.grad_ref.refs_1_, bf16[1024,896]{1,0:T(8,128)(2,1)} %weight_ref.1), custom_call_target="tpu_custom_call" | custom-call | flops 3758096384 | bytes 9699328 | tf_op jit(solution)/shard_map/partial_product/pallas_call | solution.py:35
  66.7 0.7 copy-done.6
  67.4 0.1 copy.10
  67.5 0.1 mul.37
  67.7 0.1 constant_dynamic-update-slice_fusion.3
  67.7 4.3 %collective-permute-start = (bf16[64,1024]{1,0:T(8,128)(2,1)S(1)}, bf16[64,1024]{1,0:T(8,128)(2,1)S(1)}, u32[]{:S(2)}, u32[]{:S(2)}) collective-permute-start(bf16[64,1024]{1,0:T(8,128)(2,1)S(1)} %get-tuple-element.3), channel_id=1, source_target_pairs={{0,1},{1,2},{2,3},{3,0},{4,5},{5,6},{6,7},{7,4},{8,9},{9,10},{10,1... | collective-permute-start | bytes 393224 | tf_op jit(solution)/shard_map/ppermute | solution.py:23
  72.1 3.6 %collective-permute-start.1 = (bf16[64,1024]{1,0:T(8,128)(2,1)S(1)}, bf16[64,1024]{1,0:T(8,128)(2,1)S(1)}, u32[]{:S(2)}, u32[]{:S(2)}) collective-permute-start(bf16[64,1024]{1,0:T(8,128)(2,1)S(1)} %get-tuple-element.3), channel_id=1, source_target_pairs={{0,3},{1,0},{2,1},{3,2},{4,7},{5,4},{6,5},{7,6},{8,11},{9,8},{10,9... | collective-permute-start | bytes 393224 | tf_op jit(solution)/shard_map/ppermute | solution.py:23
  75.7 6.7 %collective-permute-start.2 = (bf16[64,1024]{1,0:T(8,128)(2,1)S(1)}, bf16[64,1024]{1,0:T(8,128)(2,1)S(1)}, u32[]{:S(2)}, u32[]{:S(2)}) collective-permute-start(bf16[64,1024]{1,0:T(8,128)(2,1)S(1)} %get-tuple-element.3), channel_id=1, source_target_pairs={{0,2},{1,3},{2,0},{3,1},{4,6},{5,7},{6,4},{7,5},{8,10},{9,11},{10,... | collective-permute-start | bytes 393224 | tf_op jit(solution)/shard_map/ppermute | solution.py:23
  82.5 9.4 %collective-permute-done.2 = bf16[64,1024]{1,0:T(8,128)(2,1)S(1)} collective-permute-done((bf16[64,1024]{1,0:T(8,128)(2,1)S(1)}, bf16[64,1024]{1,0:T(8,128)(2,1)S(1)}, u32[]{:S(2)}, u32[]{:S(2)}) %collective-permute-start.2) | collective-permute-done | bytes 131104 | tf_op jit(solution)/shard_map/ppermute | solution.py:23
  91.9 5.9 %collective-permute-start.4 = (bf16[256,1024]{1,0:T(8,128)(2,1)S(1)}, bf16[256,1024]{1,0:T(8,128)(2,1)S(1)}, u32[]{:S(2)}, u32[]{:S(2)}) collective-permute-start(bf16[256,1024]{1,0:T(8,128)(2,1)S(1)} %constant_dynamic-update-slice_fusion.refs_2_), channel_id=1, source_target_pairs={{0,28},{4,0},{8,4},{12,8},{16,12},{20,16},{24,20},{28,24},{1,29},{... | collective-permute-start | bytes 1572872 | tf_op jit(solution)/shard_map/ppermute | solution.py:23
  97.8 1.9 collective-permute-start.3
  99.7 21.3 %collective-permute-done.4.refs_1_.refs_4_ = bf16[256,1024]{1,0:T(8,128)(2,1)S(1)} collective-permute-done((bf16[256,1024]{1,0:T(8,128)(2,1)S(1)}, bf16[256,1024]{1,0:T(8,128)(2,1)S(1)}, u32[]{:S(2)}, u32[]{:S(2)}) %collective-permute-start.4) | collective-permute-done | bytes 524320 | tf_op jit(solution)/shard_map/ppermute | solution.py:23
  121.0 5.6 %collective-permute-start.6 = (bf16[256,1024]{1,0:T(8,128)(2,1)S(1)}, bf16[256,1024]{1,0:T(8,128)(2,1)}, u32[]{:S(2)}, u32[]{:S(2)}) collective-permute-start(bf16[256,1024]{1,0:T(8,128)(2,1)S(1)} %collective-permute-done.4.refs_1_.refs_4_), channel_id=1, source_target_pairs={{0,28},{4,0},{8,4},{12,8},{16,12},{20,16},{24,20},{28,24},{1,29},{... | collective-permute-start | bytes 1572872 | tf_op jit(solution)/shard_map/ppermute | solution.py:23
  126.6 1.9 collective-permute-start.5
  128.5 16.7 %collective-permute-done.6.refs_6_ = bf16[256,1024]{1,0:T(8,128)(2,1)} collective-permute-done((bf16[256,1024]{1,0:T(8,128)(2,1)S(1)}, bf16[256,1024]{1,0:T(8,128)(2,1)}, u32[]{:S(2)}, u32[]{:S(2)}) %collective-permute-start.6) | collective-permute-done | bytes 524320 | tf_op jit(solution)/shard_map/ppermute | solution.py:23
  145.2 4.8 %collective-permute-start.8 = (bf16[256,1024]{1,0:T(8,128)(2,1)}, bf16[256,1024]{1,0:T(8,128)(2,1)S(1)}, u32[]{:S(2)}, u32[]{:S(2)}) collective-permute-start(bf16[256,1024]{1,0:T(8,128)(2,1)} %collective-permute-done.6.refs_6_), channel_id=1, source_target_pairs={{0,28},{4,0},{8,4},{12,8},{16,12},{20,16},{24,20},{28,24},{1,29},{... | collective-permute-start | bytes 1572872 | tf_op jit(solution)/shard_map/ppermute | solution.py:23
  150.0 1.9 collective-permute-start.7
  151.9 5.9 %all-to-all-start = ((bf16[4,64,1024]{2,1,0:T(8,128)(2,1)}), bf16[4,64,1024]{2,1,0:T(8,128)(2,1)S(1)}, u32[]{:S(2)}, u32[]{:S(2)}) async-start(bf16[4,64,1024]{2,1,0:T(8,128)(2,1)} %bitcast.11), calls=%async_computation.1 | async-start | bytes 1048576 | tf_op jit(solution)/shard_map/all_to_all | solution.py:148
  157.8 3.4 %collective-permute-done.8.refs_1_.refs_8_ = bf16[256,1024]{1,0:T(8,128)(2,1)S(1)} collective-permute-done((bf16[256,1024]{1,0:T(8,128)(2,1)}, bf16[256,1024]{1,0:T(8,128)(2,1)S(1)}, u32[]{:S(2)}, u32[]{:S(2)}) %collective-permute-start.8) | collective-permute-done | bytes 524320 | tf_op jit(solution)/shard_map/ppermute | solution.py:23
  161.2 5.5 %collective-permute-start.10 = (bf16[128,1024]{1,0:T(8,128)(2,1)S(1)}, bf16[128,1024]{1,0:T(8,128)(2,1)}, u32[]{:S(2)}, u32[]{:S(2)}) collective-permute-start(bf16[128,1024]{1,0:T(8,128)(2,1)S(1)} %slice.9), channel_id=1, source_target_pairs={{0,28},{4,0},{8,4},{12,8},{16,12},{20,16},{24,20},{28,24},{1,29},{... | collective-permute-start | bytes 786440 | tf_op jit(solution)/shard_map/ppermute | solution.py:23
  166.7 0.8 slice.8
  167.5 1.9 collective-permute-start.9
  169.4 0.6 mark.2.refs_11_
  170.0 0.6 mark.3.refs_12_
  170.6 0.5 collective-permute-done.10.refs_10_
  171.1 6.4 %collective-permute-done.9.refs_9_ = bf16[128,1024]{1,0:T(8,128)(2,1)} collective-permute-done((bf16[128,1024]{1,0:T(8,128)(2,1)}, bf16[128,1024]{1,0:T(8,128)(2,1)}, u32[]{:S(2)}, u32[]{:S(2)}) %collective-permute-start.9) | collective-permute-done | bytes 262176 | tf_op jit(solution)/shard_map/ppermute | solution.py:23
  177.6 9.2 %outer_product.1 = bf16[1024,896]{1,0:T(8,128)(2,1)} custom-call(s32[1]{0:T(128)} %bitcast.2.refs_0_, bf16[2048,896]{1,0:T(8,128)(2,1)} %all-gather.2.cloned.1.call-done.grad_ref.refs_1_, bf16[256,1024]{1,0:T(8,128)(2,1)} %copy-done.2, bf16[256,1024]{1,0:T(8,128)(2,1)} %copy-done.4, bf16[256,1024]{1,0:T(8,128)(2,1)} %copy-done.3, ...), custom_call_target="tpu_custom_call" | custom-call | flops 3758096384 | bytes 9699328 | tf_op jit(solution)/shard_map/outer_product/pallas_call | solution.py:90
  186.8 0.7 reduce_sum.12
  (29 shorter events, 0.3 us)
Async XLA Ops:
  7.2 49.6 %all-gather.2.cloned.1.call-start = ((), (), s32[]{:S(2)}) async-start(), calls=%async_computation.2 | async-start | bytes 3899392 | tf_op jit(solution)/shard_map/all_gather | solution.py:142
  9.8 142.1 %reduce-scatter.2.cloned.1.call-start = ((), (), s32[]{:S(2)}) async-start(), calls=%async_computation.3 | async-start | bytes 4718592 | tf_op jit(solution)/shard_map/reduce_scatter | solution.py:146
  66.7 0.7 copy-start.6
  66.7 1.0 copy-start.5
  67.7 14.7 %collective-permute-start = (bf16[64,1024]{1,0:T(8,128)(2,1)S(1)}, bf16[64,1024]{1,0:T(8,128)(2,1)S(1)}, u32[]{:S(2)}, u32[]{:S(2)}) collective-permute-start(bf16[64,1024]{1,0:T(8,128)(2,1)S(1)} %get-tuple-element.3), channel_id=1, source_target_pairs={{0,1},{1,2},{2,3},{3,0},{4,5},{5,6},{6,7},{7,4},{8,9},{9,10},{10,1... | collective-permute-start | bytes 393224 | tf_op jit(solution)/shard_map/ppermute | solution.py:23
  72.1 10.4 %collective-permute-start.1 = (bf16[64,1024]{1,0:T(8,128)(2,1)S(1)}, bf16[64,1024]{1,0:T(8,128)(2,1)S(1)}, u32[]{:S(2)}, u32[]{:S(2)}) collective-permute-start(bf16[64,1024]{1,0:T(8,128)(2,1)S(1)} %get-tuple-element.3), channel_id=1, source_target_pairs={{0,3},{1,0},{2,1},{3,2},{4,7},{5,4},{6,5},{7,6},{8,11},{9,8},{10,9... | collective-permute-start | bytes 393224 | tf_op jit(solution)/shard_map/ppermute | solution.py:23
  75.7 16.2 %collective-permute-start.2 = (bf16[64,1024]{1,0:T(8,128)(2,1)S(1)}, bf16[64,1024]{1,0:T(8,128)(2,1)S(1)}, u32[]{:S(2)}, u32[]{:S(2)}) collective-permute-start(bf16[64,1024]{1,0:T(8,128)(2,1)S(1)} %get-tuple-element.3), channel_id=1, source_target_pairs={{0,2},{1,3},{2,0},{3,1},{4,6},{5,7},{6,4},{7,5},{8,10},{9,11},{10,... | collective-permute-start | bytes 393224 | tf_op jit(solution)/shard_map/ppermute | solution.py:23
  91.9 85.7 %copy-start.2 = (bf16[256,1024]{1,0:T(8,128)(2,1)}, bf16[256,1024]{1,0:T(8,128)(2,1)S(1)}, u32[]{:S(2)}) copy-start(bf16[256,1024]{1,0:T(8,128)(2,1)S(1)} %constant_dynamic-update-slice_fusion.refs_2_) | copy-start | bytes 1572868
  91.9 29.0 %collective-permute-start.4 = (bf16[256,1024]{1,0:T(8,128)(2,1)S(1)}, bf16[256,1024]{1,0:T(8,128)(2,1)S(1)}, u32[]{:S(2)}, u32[]{:S(2)}) collective-permute-start(bf16[256,1024]{1,0:T(8,128)(2,1)S(1)} %constant_dynamic-update-slice_fusion.refs_2_), channel_id=1, source_target_pairs={{0,28},{4,0},{8,4},{12,8},{16,12},{20,16},{24,20},{28,24},{1,29},{... | collective-permute-start | bytes 1572872 | tf_op jit(solution)/shard_map/ppermute | solution.py:23
  97.8 28.8 %collective-permute-start.3 = (bf16[256,1024]{1,0:T(8,128)(2,1)S(1)}, bf16[256,1024]{1,0:T(8,128)(2,1)S(1)}, u32[]{:S(2)}, u32[]{:S(2)}) collective-permute-start(bf16[256,1024]{1,0:T(8,128)(2,1)S(1)} %constant_dynamic-update-slice_fusion.refs_2_), channel_id=1, source_target_pairs={{0,4},{4,8},{8,12},{12,16},{16,20},{20,24},{24,28},{28,0},{1,5},{5... | collective-permute-start | bytes 1572872 | tf_op jit(solution)/shard_map/ppermute | solution.py:23
  121.0 48.5 %copy-start.3 = (bf16[256,1024]{1,0:T(8,128)(2,1)}, bf16[256,1024]{1,0:T(8,128)(2,1)S(1)}, u32[]{:S(2)}) copy-start(bf16[256,1024]{1,0:T(8,128)(2,1)S(1)} %collective-permute-done.4.refs_1_.refs_4_) | copy-start | bytes 1572868
  121.0 24.2 %collective-permute-start.6 = (bf16[256,1024]{1,0:T(8,128)(2,1)S(1)}, bf16[256,1024]{1,0:T(8,128)(2,1)}, u32[]{:S(2)}, u32[]{:S(2)}) collective-permute-start(bf16[256,1024]{1,0:T(8,128)(2,1)S(1)} %collective-permute-done.4.refs_1_.refs_4_), channel_id=1, source_target_pairs={{0,28},{4,0},{8,4},{12,8},{16,12},{20,16},{24,20},{28,24},{1,29},{... | collective-permute-start | bytes 1572872 | tf_op jit(solution)/shard_map/ppermute | solution.py:23
  126.6 42.9 %copy-start.4 = (bf16[256,1024]{1,0:T(8,128)(2,1)}, bf16[256,1024]{1,0:T(8,128)(2,1)S(1)}, u32[]{:S(2)}) copy-start(bf16[256,1024]{1,0:T(8,128)(2,1)S(1)} %collective-permute-done.3.refs_0_.refs_3_) | copy-start | bytes 1572868
  126.6 23.4 %collective-permute-start.5 = (bf16[256,1024]{1,0:T(8,128)(2,1)S(1)}, bf16[256,1024]{1,0:T(8,128)(2,1)}, u32[]{:S(2)}, u32[]{:S(2)}) collective-permute-start(bf16[256,1024]{1,0:T(8,128)(2,1)S(1)} %collective-permute-done.3.refs_0_.refs_3_), channel_id=1, source_target_pairs={{0,4},{4,8},{8,12},{12,16},{16,20},{20,24},{24,28},{28,0},{1,5},{5... | collective-permute-start | bytes 1572872 | tf_op jit(solution)/shard_map/ppermute | solution.py:23
  145.2 16.0 %collective-permute-start.8 = (bf16[256,1024]{1,0:T(8,128)(2,1)}, bf16[256,1024]{1,0:T(8,128)(2,1)S(1)}, u32[]{:S(2)}, u32[]{:S(2)}) collective-permute-start(bf16[256,1024]{1,0:T(8,128)(2,1)} %collective-permute-done.6.refs_6_), channel_id=1, source_target_pairs={{0,28},{4,0},{8,4},{12,8},{16,12},{20,16},{24,20},{28,24},{1,29},{... | collective-permute-start | bytes 1572872 | tf_op jit(solution)/shard_map/ppermute | solution.py:23
  150.0 16.7 %collective-permute-start.7 = (bf16[256,1024]{1,0:T(8,128)(2,1)}, bf16[256,1024]{1,0:T(8,128)(2,1)S(1)}, u32[]{:S(2)}, u32[]{:S(2)}) collective-permute-start(bf16[256,1024]{1,0:T(8,128)(2,1)} %collective-permute-done.5.refs_5_), channel_id=1, source_target_pairs={{0,4},{4,8},{8,12},{12,16},{16,20},{20,24},{24,28},{28,0},{1,5},{5... | collective-permute-start | bytes 1572872 | tf_op jit(solution)/shard_map/ppermute | solution.py:23
  151.9 34.8 %all-to-all-start = ((bf16[4,64,1024]{2,1,0:T(8,128)(2,1)}), bf16[4,64,1024]{2,1,0:T(8,128)(2,1)S(1)}, u32[]{:S(2)}, u32[]{:S(2)}) async-start(bf16[4,64,1024]{2,1,0:T(8,128)(2,1)} %bitcast.11), calls=%async_computation.1 | async-start | bytes 1048576 | tf_op jit(solution)/shard_map/all_to_all | solution.py:148
  161.2 8.9 %copy-start = (bf16[256,1024]{1,0:T(8,128)(2,1)}, bf16[256,1024]{1,0:T(8,128)(2,1)S(1)}, u32[]{:S(2)}) copy-start(bf16[256,1024]{1,0:T(8,128)(2,1)S(1)} %collective-permute-done.8.refs_1_.refs_8_) | copy-start | bytes 1572868
  161.2 9.9 %collective-permute-start.10 = (bf16[128,1024]{1,0:T(8,128)(2,1)S(1)}, bf16[128,1024]{1,0:T(8,128)(2,1)}, u32[]{:S(2)}, u32[]{:S(2)}) collective-permute-start(bf16[128,1024]{1,0:T(8,128)(2,1)S(1)} %slice.9), channel_id=1, source_target_pairs={{0,28},{4,0},{8,4},{12,8},{16,12},{20,16},{24,20},{28,24},{1,29},{... | collective-permute-start | bytes 786440 | tf_op jit(solution)/shard_map/ppermute | solution.py:23
  166.7 3.3 %copy-start.1 = (bf16[256,1024]{1,0:T(8,128)(2,1)}, bf16[256,1024]{1,0:T(8,128)(2,1)S(1)}, u32[]{:S(2)}) copy-start(bf16[256,1024]{1,0:T(8,128)(2,1)S(1)} %collective-permute-done.7.refs_0_.refs_7_) | copy-start | bytes 1572868
  167.5 10.1 %collective-permute-start.9 = (bf16[128,1024]{1,0:T(8,128)(2,1)}, bf16[128,1024]{1,0:T(8,128)(2,1)}, u32[]{:S(2)}, u32[]{:S(2)}) collective-permute-start(bf16[128,1024]{1,0:T(8,128)(2,1)} %slice.8), channel_id=1, source_target_pairs={{0,4},{4,8},{8,12},{12,16},{16,20},{20,24},{24,28},{28,0},{1,5},{5... | collective-permute-start | bytes 786440 | tf_op jit(solution)/shard_map/ppermute | solution.py:23
Sparse Core Ops, SparseCore 0:
  10.7 46.0 all-gather.1
  66.9 76.9 reduce-scatter.1

commit v2 on v0

v2 whole, which is shorter than its diff:
```python
import jax
import jax.numpy as jnp
from jax import lax
from jax.experimental import pallas as pl
from jax.experimental.pallas import tpu as pltpu
from jax.sharding import Mesh, PartitionSpec as P


QB = 128
NY = 4
NZ = 8
ROW = ("ylo", "x", "core")
COL = ("z", "yhi")


def dequantize(values, scales):
    height, breadth = values.shape
    scaled = values.astype(jnp.float32).reshape(height, breadth // QB, QB) * scales[:, :, None]
    return scaled.reshape(height, breadth).astype(jnp.bfloat16)


def shift(array, axis, size, by):
    return lax.ppermute(array, axis, [(i, (i + by) % size) for i in range(size)])


def mark_kernel(*refs):
    refs[-1][...] = jnp.zeros_like(refs[-1])


def mark(*arrays):
    return pl.pallas_call(
        mark_kernel,
        in_specs=[pl.BlockSpec(memory_space=pl.ANY)] * len(arrays),
        out_shape=jax.ShapeDtypeStruct((8, 128), jnp.float32),
        cost_estimate=pl.CostEstimate(flops=0, bytes_accessed=4096, transcendentals=0),
        name="mark",
    )(*arrays)


def partial_kernel(grad_ref, weight_ref, *refs):
    out_ref = refs[-1]
    out_ref[...] = lax.dot_general(
        grad_ref[...], weight_ref[...], (((1,), (1,)), ((), ())), preferred_element_type=jnp.float32
    ).astype(out_ref.dtype)


def partial_product(gradients, weight, marks, tile=256):
    tokens, hidden = gradients.shape
    width = weight.shape[0]
    return pl.pallas_call(
        partial_kernel,
        grid=(tokens // tile,),
        in_specs=[
            pl.BlockSpec((tile, hidden), lambda i: (i, 0)),
            pl.BlockSpec((width, hidden), lambda i: (0, 0)),
        ]
        + [pl.BlockSpec(memory_space=pl.ANY)] * len(marks),
        out_specs=pl.BlockSpec((tile, width), lambda i: (i, 0)),
        out_shape=jax.ShapeDtypeStruct((tokens, width), jnp.bfloat16),
        cost_estimate=pl.CostEstimate(
            flops=2 * tokens * hidden * width,
            bytes_accessed=2 * (tokens * hidden + hidden * width + tokens * width),
            transcendentals=0,
        ),
        name="partial_product",
    )(gradients, weight, *marks)


def outer_kernel(keys, rows, place_ref, grad_ref, *refs):
    out_ref, acts_ref = refs[-2:]
    z, y = place_ref[0], place_ref[1]
    for key, act_ref in zip(keys, refs):
        for j, (hop, lane) in enumerate(key):
            start = (((z + hop) & (NZ - 1)) * NY + ((y + lane) & (NY - 1))) * rows
            acts_ref[pl.ds(pl.multiple_of(start, rows), rows), :] = act_ref[j * rows : (j + 1) * rows, :]
    out_ref[...] = lax.dot_general(
        acts_ref[...], grad_ref[...], (((0,), (0,)), ((), ())), preferred_element_type=jnp.float32
    ).astype(out_ref.dtype)


def outer_product(place, gradients, held, marks, tile=256):
    tokens, hidden = gradients.shape
    width = held[0][1].shape[1]
    keys = [key for key, _ in held]
    arrays = [array for _, array in held]

    def kernel(*refs):
        outer_kernel(keys, tokens // (NZ * NY), *refs[: 2 + len(arrays)], *refs[-2:])

    return pl.pallas_call(
        kernel,
        grid=(width // tile,),
        in_specs=[
            pl.BlockSpec(memory_space=pltpu.SMEM),
            pl.BlockSpec((tokens, hidden), lambda i: (0, 0)),
        ]
        + [pl.BlockSpec((array.shape[0], tile), lambda i: (0, i)) for array in arrays]
        + [pl.BlockSpec(memory_space=pl.ANY)] * len(marks),
        out_specs=pl.BlockSpec((tile, hidden), lambda i: (i, 0)),
        out_shape=jax.ShapeDtypeStruct((width, hidden), jnp.bfloat16),
        scratch_shapes=[pltpu.VMEM((tokens, tile), jnp.bfloat16)],
        cost_estimate=pl.CostEstimate(
            flops=2 * tokens * hidden * width,
            bytes_accessed=2 * (tokens * hidden + hidden * width + tokens * width),
            transcendentals=0,
        ),
        name="outer_product",
    )(place, gradients, *arrays, *marks)


def gather_acts(local):
    rows = local.shape[0]
    opposite = shift(local, "yhi", NY, NY // 2)
    ups, downs = [jnp.concatenate([local, opposite], axis=0)], []
    downs.append(ups[0])
    for _ in range(1, NZ // 2):
        ups.append(shift(ups[-1], "z", NZ, 1))
        downs.append(shift(downs[-1], "z", NZ, -1))
    ups.append(shift(ups[-1], "z", NZ, 1))
    ring = [(0, ups[0])]
    for step in range(1, NZ // 2):
        ring += [(-step, ups[step]), (step, downs[step])]
    ring.append((NZ // 2, ups[-1]))
    column = jnp.concatenate([array[:rows] for _, array in ring], axis=0)
    left = shift(column, "yhi", NY, 1)
    right = shift(column, "yhi", NY, -1)
    hops = [hop for hop, _ in ring]
    held = [([(hop, -1) for hop in hops], left), ([(hop, 1) for hop in hops], right)]
    held += [([(hop, 0), (hop, NY // 2)], array) for hop, array in ring]
    return held, [mark(ups[2], downs[2])]


def shards(act_values, act_scales, grad_values, grad_scales, weight):
    place = jnp.stack([lax.axis_index("z"), lax.axis_index("yhi")]).astype(jnp.int32)
    rows = act_values.shape[0]
    grad_local = dequantize(grad_values, grad_scales)
    gradients = lax.all_gather(grad_local, ROW, axis=0, tiled=True)
    held, marks = gather_acts(dequantize(act_values, act_scales))
    partial = partial_product(gradients, weight, [])
    over_z = lax.psum_scatter(partial, "z", scatter_dimension=0, tiled=True)
    blocks = lax.all_to_all(over_z, "yhi", 0, 0, tiled=True).reshape(NY, rows, -1)
    summed = jnp.sum(blocks.astype(jnp.float32), axis=0).astype(jnp.bfloat16)
    weight_grad = outer_product(place, gradients, held, marks)
    return (summed, weight_grad)


def solution(mesh):
    fine = Mesh(mesh.devices.reshape(2, 4, 2, NZ, NY), ROW + COL)
    placed = (P(COL, ROW), P(COL, ROW), P(ROW, COL), P(ROW, COL), P(ROW, COL))
    return jax.shard_map(
        shards,
        mesh=fine,
        in_specs=placed,
        out_specs=(P(COL, ROW), P(ROW, COL)),
        check_vma=False,
    )
```

time: 412 us -> 229 us (0.56)
  the two profiles are of different devices: /device:TPU:2 before, /device:TPU:10 now
where the time goes in v2:
time: 229 us; the launch traced here: 228 us
  waiting for transfers between devices  139 us (61%)
  starting transfers between devices  45.3 us (20%)
  Pallas kernels  19.6 us (9%)
  between operations  14.2 us (6%)
  local copies, waits for them, and re-layouts  6.59 us (3%)
  other arithmetic  3.8 us (2%)
    ppermute x10, waiting for transfers between devices, shift(): lax.ppermute(array, axis, [(i, (i + by) % size) for i in range(size)])  92.4 us
    all_gather x1, waiting for transfers between devices, shards(): gradients = lax.all_gather(grad_local, ROW, axis=0, tiled=True)  46.3 us
    ppermute x10, starting transfers between devices, shift(): lax.ppermute(array, axis, [(i, (i + by) % size) for i in range(size)])  38.5 us
    pallas_call x1, Pallas kernels, partial_product(): pl.pallas_call(partial_kernel, grid=(tokens // tile,), in_specs=[pl.Block...  9.94 us
    pallas_call x1, Pallas kernels, outer_product(): pl.pallas_call(kernel, grid=(width // tile,), in_specs=[pl.BlockSpec(memo...  9.11 us
    all_to_all x1, starting transfers between devices, shards(): lax.all_to_all(over_z, 'yhi', 0, 0, tiled=True).reshape(NY, rows, -1)  6.65 us
    unnamed x27, local copies, waits for them, and re-layouts  4.85 us
  transfers between devices with their start and end apart: 13, of which 10 were waited for; matrix products, arithmetic and copies ran while one was open for 3% of the time, Pallas kernels for 4%

profile of v2, /device:TPU:10, one launch (start us, length us, event | category | flops | bytes accessed | tf_op | source)
XLA Modules:
  0.0 228.3 jit_solution(16305374330409191775)
XLA Ops:
  7.2 0.7 mul.22
  8.1 1.7 multiply_convert_fusion
  9.9 46.3 %all-gather.2.cloned.1.call-done.grad_ref.refs_1_ = bf16[2048,896]{1,0:T(8,128)(2,1)} async-done(((bf16[128,896]{1,0:T(8,128)(2,1)}), bf16[2048,896]{1,0:T(8,128)(2,1)}) %all-gather.2.cloned.1.call-update) | async-done | bytes 3670032 | tf_op jit(solution)/shard_map/all_gather | solution.py:137
  56.1 9.9 %partial_product.1 = bf16[2048,1024]{1,0:T(8,128)(2,1)} custom-call(bf16[2048,896]{1,0:T(8,128)(2,1)} %all-gather.2.cloned.1.call-done.grad_ref.refs_1_, bf16[1024,896]{1,0:T(8,128)(2,1)} %weight_ref.1), custom_call_target="tpu_custom_call" | custom-call | flops 3758096384 | bytes 9699328 | tf_op jit(solution)/shard_map/partial_product/pallas_call | solution.py:50
  67.0 0.7 constant_dynamic-update-slice_fusion
  67.7 7.0 %collective-permute-start = (bf16[64,1024]{1,0:T(8,128)(2,1)S(1)}, bf16[64,1024]{1,0:T(8,128)(2,1)S(1)}, u32[]{:S(2)}, u32[]{:S(2)}) collective-permute-start(bf16[64,1024]{1,0:T(8,128)(2,1)S(1)} %get-tuple-element.3), channel_id=1, source_target_pairs={{0,2},{1,3},{2,0},{3,1},{4,6},{5,7},{6,4},{7,5},{8,10},{9,11},{10,... | collective-permute-start | bytes 393224 | tf_op jit(solution)/shard_map/ppermute | solution.py:23
  74.8 7.2 %collective-permute-done = bf16[64,1024]{1,0:T(8,128)(2,1)S(1)} collective-permute-done((bf16[64,1024]{1,0:T(8,128)(2,1)S(1)}, bf16[64,1024]{1,0:T(8,128)(2,1)S(1)}, u32[]{:S(2)}, u32[]{:S(2)}) %collective-permute-start) | collective-permute-done | bytes 131104 | tf_op jit(solution)/shard_map/ppermute | solution.py:23
  82.0 5.9 %collective-permute-start.2 = (bf16[128,1024]{1,0:T(8,128)(2,1)S(1)}, bf16[128,1024]{1,0:T(8,128)(2,1)S(1)}, u32[]{:S(2)}, u32[]{:S(2)}) collective-permute-start(bf16[128,1024]{1,0:T(8,128)(2,1)S(1)} %pad_maximum_fusion.refs_4_), channel_id=1, source_target_pairs={{0,28},{4,0},{8,4},{12,8},{16,12},{20,16},{24,20},{28,24},{1,29},{... | collective-permute-start | bytes 786440 | tf_op jit(solution)/shard_map/ppermute | solution.py:23
  87.8 1.9 collective-permute-start.1
  89.8 9.4 %collective-permute-done.2.refs_6_ = bf16[128,1024]{1,0:T(8,128)(2,1)S(1)} collective-permute-done((bf16[128,1024]{1,0:T(8,128)(2,1)S(1)}, bf16[128,1024]{1,0:T(8,128)(2,1)S(1)}, u32[]{:S(2)}, u32[]{:S(2)}) %collective-permute-start.2) | collective-permute-done | bytes 262176 | tf_op jit(solution)/shard_map/ppermute | solution.py:23
  99.2 5.6 %collective-permute-start.4 = (bf16[128,1024]{1,0:T(8,128)(2,1)S(1)}, bf16[128,1024]{1,0:T(8,128)(2,1)S(1)}, u32[]{:S(2)}, u32[]{:S(2)}) collective-permute-start(bf16[128,1024]{1,0:T(8,128)(2,1)S(1)} %collective-permute-done.2.refs_6_), channel_id=1, source_target_pairs={{0,28},{4,0},{8,4},{12,8},{16,12},{20,16},{24,20},{28,24},{1,29},{... | collective-permute-start | bytes 786440 | tf_op jit(solution)/shard_map/ppermute | solution.py:23
  105.2 1.9 collective-permute-start.3
  107.1 0.7 slice_dynamic-update-slice_fusion.6
  107.7 0.7 slice_dynamic-update-slice_fusion.5
  108.4 7.7 %collective-permute-done.4.refs_1_.refs_8_ = bf16[128,1024]{1,0:T(8,128)(2,1)S(1)} collective-permute-done((bf16[128,1024]{1,0:T(8,128)(2,1)S(1)}, bf16[128,1024]{1,0:T(8,128)(2,1)S(1)}, u32[]{:S(2)}, u32[]{:S(2)}) %collective-permute-start.4) | collective-permute-done | bytes 262176 | tf_op jit(solution)/shard_map/ppermute | solution.py:23
  116.1 5.6 %collective-permute-start.6 = (bf16[128,1024]{1,0:T(8,128)(2,1)S(1)}, bf16[128,1024]{1,0:T(8,128)(2,1)S(1)}, u32[]{:S(2)}, u32[]{:S(2)}) collective-permute-start(bf16[128,1024]{1,0:T(8,128)(2,1)S(1)} %collective-permute-done.4.refs_1_.refs_8_), channel_id=1, source_target_pairs={{0,28},{4,0},{8,4},{12,8},{16,12},{20,16},{24,20},{28,24},{1,29},{... | collective-permute-start | bytes 786440 | tf_op jit(solution)/shard_map/ppermute | solution.py:23
  122.3 1.9 collective-permute-start.5
  124.2 0.7 slice_dynamic-update-slice_fusion.4
  124.8 0.7 slice_dynamic-update-slice_fusion.3
  125.5 13.6 %collective-permute-done.5.refs_9_ = bf16[128,1024]{1,0:T(8,128)(2,1)S(1)} collective-permute-done((bf16[128,1024]{1,0:T(8,128)(2,1)S(1)}, bf16[128,1024]{1,0:T(8,128)(2,1)S(1)}, u32[]{:S(2)}, u32[]{:S(2)}) %collective-permute-start.5) | collective-permute-done | bytes 262176 | tf_op jit(solution)/shard_map/ppermute | solution.py:23
  139.1 1.9 collective-permute-start.7
  141.1 0.7 slice_dynamic-update-slice_fusion.2
  141.7 0.7 slice_dynamic-update-slice_fusion.1
  142.5 6.2 %collective-permute-done.7.refs_11_ = bf16[128,1024]{1,0:T(8,128)(2,1)S(1)} collective-permute-done((bf16[128,1024]{1,0:T(8,128)(2,1)S(1)}, bf16[128,1024]{1,0:T(8,128)(2,1)S(1)}, u32[]{:S(2)}, u32[]{:S(2)}) %collective-permute-start.7) | collective-permute-done | bytes 262176 | tf_op jit(solution)/shard_map/ppermute | solution.py:23
  148.6 0.7 slice_dynamic-update-slice_fusion
  149.3 4.9 %collective-permute-start.9 = (bf16[512,1024]{1,0:T(8,128)(2,1)}, bf16[512,1024]{1,0:T(8,128)(2,1)}, u32[]{:S(2)}, u32[]{:S(2)}) collective-permute-start(bf16[512,1024]{1,0:T(8,128)(2,1)} %slice_dynamic-update-slice_fusion), channel_id=1, source_target_pairs={{0,3},{1,0},{2,1},{3,2},{4,7},{5,4},{6,5},{7,6},{8,11},{9,8},{10,9... | collective-permute-start | bytes 3145736 | tf_op jit(solution)/shard_map/ppermute | solution.py:23
  154.2 1.9 collective-permute-start.8
  156.2 6.7 %all-to-all-start = ((bf16[4,64,1024]{2,1,0:T(8,128)(2,1)}), bf16[4,64,1024]{2,1,0:T(8,128)(2,1)S(1)}, u32[]{:S(2)}, u32[]{:S(2)}) async-start(bf16[4,64,1024]{2,1,0:T(8,128)(2,1)} %bitcast.12), calls=%async_computation.1 | async-start | bytes 1048576 | tf_op jit(solution)/shard_map/all_to_all | solution.py:141
  164.1 24.0 %collective-permute-done.9.refs_3_ = bf16[512,1024]{1,0:T(8,128)(2,1)} collective-permute-done((bf16[512,1024]{1,0:T(8,128)(2,1)}, bf16[512,1024]{1,0:T(8,128)(2,1)}, u32[]{:S(2)}, u32[]{:S(2)}) %collective-permute-start.9) | collective-permute-done | bytes 1048608 | tf_op jit(solution)/shard_map/ppermute | solution.py:23
  188.1 23.5 %collective-permute-done.8.refs_2_ = bf16[512,1024]{1,0:T(8,128)(2,1)} collective-permute-done((bf16[512,1024]{1,0:T(8,128)(2,1)}, bf16[512,1024]{1,0:T(8,128)(2,1)}, u32[]{:S(2)}, u32[]{:S(2)}) %collective-permute-start.8) | collective-permute-done | bytes 1048608 | tf_op jit(solution)/shard_map/ppermute | solution.py:23
  211.6 9.1 %outer_product.1 = bf16[1024,896]{1,0:T(8,128)(2,1)} custom-call(s32[2]{0:T(128)} %pad_add_fusion.refs_0_, bf16[2048,896]{1,0:T(8,128)(2,1)} %all-gather.2.cloned.1.call-done.grad_ref.refs_1_, bf16[512,1024]{1,0:T(8,128)(2,1)} %collective-permute-done.8.refs_2_, bf16[512,1024]{1,0:T(8,128)(2,1)} %collective-permute-done.9.refs_3_, ...), custom_call_target="tpu_custom_call" | custom-call | flops 3758096384 | bytes 9699328 | tf_op jit(solution)/shard_map/outer_product/pallas_call | solution.py:90
  220.7 0.7 reduce_sum.12
  (35 shorter events, 3.4 us)
Async XLA Ops:
  7.2 49.0 %all-gather.2.cloned.1.call-start = ((), (), s32[]{:S(2)}) async-start(), calls=%async_computation.2 | async-start | bytes 3899392 | tf_op jit(solution)/shard_map/all_gather | solution.py:137
  9.8 146.3 %reduce-scatter.2.cloned.1.call-start = ((), (), s32[]{:S(2)}) async-start(), calls=%async_computation.3 | async-start | bytes 4718592 | tf_op jit(solution)/shard_map/reduce_scatter | solution.py:140
  66.1 0.7 copy-start.9
  66.1 0.9 copy-start.3
  67.7 14.2 %collective-permute-start = (bf16[64,1024]{1,0:T(8,128)(2,1)S(1)}, bf16[64,1024]{1,0:T(8,128)(2,1)S(1)}, u32[]{:S(2)}, u32[]{:S(2)}) collective-permute-start(bf16[64,1024]{1,0:T(8,128)(2,1)S(1)} %get-tuple-element.3), channel_id=1, source_target_pairs={{0,2},{1,3},{2,0},{3,1},{4,6},{5,7},{6,4},{7,5},{8,10},{9,11},{10,... | collective-permute-start | bytes 393224 | tf_op jit(solution)/shard_map/ppermute | solution.py:23
  81.9 129.6 %copy-start.2 = (bf16[128,1024]{1,0:T(8,128)(2,1)}, bf16[128,1024]{1,0:T(8,128)(2,1)S(1)}, u32[]{:S(2)}) copy-start(bf16[128,1024]{1,0:T(8,128)(2,1)S(1)} %pad_maximum_fusion.refs_4_) | copy-start | bytes 786436
  82.0 17.3 %collective-permute-start.2 = (bf16[128,1024]{1,0:T(8,128)(2,1)S(1)}, bf16[128,1024]{1,0:T(8,128)(2,1)S(1)}, u32[]{:S(2)}, u32[]{:S(2)}) collective-permute-start(bf16[128,1024]{1,0:T(8,128)(2,1)S(1)} %pad_maximum_fusion.refs_4_), channel_id=1, source_target_pairs={{0,28},{4,0},{8,4},{12,8},{16,12},{20,16},{24,20},{28,24},{1,29},{... | collective-permute-start | bytes 786440 | tf_op jit(solution)/shard_map/ppermute | solution.py:23
  87.8 17.3 %collective-permute-start.1 = (bf16[128,1024]{1,0:T(8,128)(2,1)S(1)}, bf16[128,1024]{1,0:T(8,128)(2,1)S(1)}, u32[]{:S(2)}, u32[]{:S(2)}) collective-permute-start(bf16[128,1024]{1,0:T(8,128)(2,1)S(1)} %pad_maximum_fusion.refs_4_), channel_id=1, source_target_pairs={{0,4},{4,8},{8,12},{12,16},{16,20},{20,24},{24,28},{28,0},{1,5},{5... | collective-permute-start | bytes 786440 | tf_op jit(solution)/shard_map/ppermute | solution.py:23
  99.2 112.3 %copy-start.4 = (bf16[128,1024]{1,0:T(8,128)(2,1)}, bf16[128,1024]{1,0:T(8,128)(2,1)S(1)}, u32[]{:S(2)}) copy-start(bf16[128,1024]{1,0:T(8,128)(2,1)S(1)} %collective-permute-done.2.refs_6_) | copy-start | bytes 786436
  99.2 16.9 %collective-permute-start.4 = (bf16[128,1024]{1,0:T(8,128)(2,1)S(1)}, bf16[128,1024]{1,0:T(8,128)(2,1)S(1)}, u32[]{:S(2)}, u32[]{:S(2)}) collective-permute-start(bf16[128,1024]{1,0:T(8,128)(2,1)S(1)} %collective-permute-done.2.refs_6_), channel_id=1, source_target_pairs={{0,28},{4,0},{8,4},{12,8},{16,12},{20,16},{24,20},{28,24},{1,29},{... | collective-permute-start | bytes 786440 | tf_op jit(solution)/shard_map/ppermute | solution.py:23
  105.1 106.4 %copy-start.5 = (bf16[128,1024]{1,0:T(8,128)(2,1)}, bf16[128,1024]{1,0:T(8,128)(2,1)S(1)}, u32[]{:S(2)}) copy-start(bf16[128,1024]{1,0:T(8,128)(2,1)S(1)} %collective-permute-done.1.refs_5_) | copy-start | bytes 786436
  105.2 17.1 %collective-permute-start.3 = (bf16[128,1024]{1,0:T(8,128)(2,1)S(1)}, bf16[128,1024]{1,0:T(8,128)(2,1)S(1)}, u32[]{:S(2)}, u32[]{:S(2)}) collective-permute-start(bf16[128,1024]{1,0:T(8,128)(2,1)S(1)} %collective-permute-done.1.refs_5_), channel_id=1, source_target_pairs={{0,4},{4,8},{8,12},{12,16},{16,20},{20,24},{24,28},{28,0},{1,5},{5... | collective-permute-start | bytes 786440 | tf_op jit(solution)/shard_map/ppermute | solution.py:23
  116.1 47.4 %copy-start = (bf16[128,1024]{1,0:T(8,128)(2,1)}, bf16[128,1024]{1,0:T(8,128)(2,1)S(1)}, u32[]{:S(2)}) copy-start(bf16[128,1024]{1,0:T(8,128)(2,1)S(1)} %collective-permute-done.4.refs_1_.refs_8_) | copy-start | bytes 786436
  116.1 25.7 %collective-permute-start.6 = (bf16[128,1024]{1,0:T(8,128)(2,1)S(1)}, bf16[128,1024]{1,0:T(8,128)(2,1)S(1)}, u32[]{:S(2)}, u32[]{:S(2)}) collective-permute-start(bf16[128,1024]{1,0:T(8,128)(2,1)S(1)} %collective-permute-done.4.refs_1_.refs_8_), channel_id=1, source_target_pairs={{0,28},{4,0},{8,4},{12,8},{16,12},{20,16},{24,20},{28,24},{1,29},{... | collective-permute-start | bytes 786440 | tf_op jit(solution)/shard_map/ppermute | solution.py:23
  122.2 41.2 %copy-start.1 = (bf16[128,1024]{1,0:T(8,128)(2,1)}, bf16[128,1024]{1,0:T(8,128)(2,1)S(1)}, u32[]{:S(2)}) copy-start(bf16[128,1024]{1,0:T(8,128)(2,1)S(1)} %collective-permute-done.3.refs_0_.refs_7_) | copy-start | bytes 786436
  122.3 16.9 %collective-permute-start.5 = (bf16[128,1024]{1,0:T(8,128)(2,1)S(1)}, bf16[128,1024]{1,0:T(8,128)(2,1)S(1)}, u32[]{:S(2)}, u32[]{:S(2)}) collective-permute-start(bf16[128,1024]{1,0:T(8,128)(2,1)S(1)} %collective-permute-done.3.refs_0_.refs_7_), channel_id=1, source_target_pairs={{0,4},{4,8},{8,12},{12,16},{16,20},{20,24},{24,28},{28,0},{1,5},{5... | collective-permute-start | bytes 786440 | tf_op jit(solution)/shard_map/ppermute | solution.py:23
  139.1 72.4 %copy-start.7 = (bf16[128,1024]{1,0:T(8,128)(2,1)}, bf16[128,1024]{1,0:T(8,128)(2,1)S(1)}, u32[]{:S(2)}) copy-start(bf16[128,1024]{1,0:T(8,128)(2,1)S(1)} %collective-permute-done.5.refs_9_) | copy-start | bytes 786436
  139.1 9.5 %collective-permute-start.7 = (bf16[128,1024]{1,0:T(8,128)(2,1)S(1)}, bf16[128,1024]{1,0:T(8,128)(2,1)S(1)}, u32[]{:S(2)}, u32[]{:S(2)}) collective-permute-start(bf16[128,1024]{1,0:T(8,128)(2,1)S(1)} %collective-permute-done.5.refs_9_), channel_id=1, source_target_pairs={{0,4},{4,8},{8,12},{12,16},{16,20},{20,24},{24,28},{28,0},{1,5},{5... | collective-permute-start | bytes 786440 | tf_op jit(solution)/shard_map/ppermute | solution.py:23
  141.7 69.8 %copy-start.6 = (bf16[128,1024]{1,0:T(8,128)(2,1)}, bf16[128,1024]{1,0:T(8,128)(2,1)S(1)}, u32[]{:S(2)}) copy-start(bf16[128,1024]{1,0:T(8,128)(2,1)S(1)} %collective-permute-done.6.refs_10_) | copy-start | bytes 786436
  148.6 62.9 %copy-start.8 = (bf16[128,1024]{1,0:T(8,128)(2,1)}, bf16[128,1024]{1,0:T(8,128)(2,1)S(1)}, u32[]{:S(2)}) copy-start(bf16[128,1024]{1,0:T(8,128)(2,1)S(1)} %collective-permute-done.7.refs_11_) | copy-start | bytes 786436
  149.3 38.7 %collective-permute-start.9 = (bf16[512,1024]{1,0:T(8,128)(2,1)}, bf16[512,1024]{1,0:T(8,128)(2,1)}, u32[]{:S(2)}, u32[]{:S(2)}) collective-permute-start(bf16[512,1024]{1,0:T(8,128)(2,1)} %slice_dynamic-update-slice_fusion), channel_id=1, source_target_pairs={{0,3},{1,0},{2,1},{3,2},{4,7},{5,4},{6,5},{7,6},{8,11},{9,8},{10,9... | collective-permute-start | bytes 3145736 | tf_op jit(solution)/shard_map/ppermute | solution.py:23
  154.2 57.3 %collective-permute-start.8 = (bf16[512,1024]{1,0:T(8,128)(2,1)}, bf16[512,1024]{1,0:T(8,128)(2,1)}, u32[]{:S(2)}, u32[]{:S(2)}) collective-permute-start(bf16[512,1024]{1,0:T(8,128)(2,1)} %slice_dynamic-update-slice_fusion), channel_id=1, source_target_pairs={{0,1},{1,2},{2,3},{3,0},{4,5},{5,6},{6,7},{7,4},{8,9},{9,10},{10,1... | collective-permute-start | bytes 3145736 | tf_op jit(solution)/shard_map/ppermute | solution.py:23
  156.2 64.5 %all-to-all-start = ((bf16[4,64,1024]{2,1,0:T(8,128)(2,1)}), bf16[4,64,1024]{2,1,0:T(8,128)(2,1)S(1)}, u32[]{:S(2)}, u32[]{:S(2)}) async-start(bf16[4,64,1024]{2,1,0:T(8,128)(2,1)} %bitcast.12), calls=%async_computation.1 | async-start | bytes 1048576 | tf_op jit(solution)/shard_map/all_to_all | solution.py:141
Sparse Core Ops, SparseCore 0:
  10.7 45.4 all-gather.1
  66.2 76.6 reduce-scatter.1

commit v3 on v2

--- a/solution.py
+++ b/solution.py
@@ -13,10 +13,20 @@
 COL = ("z", "yhi")
 
 
+def dequantize_kernel(values_ref, scales_ref, out_ref):
+    scales = scales_ref[...].T
+    for j in range(scales.shape[1]):
+        part = slice(j * QB, (j + 1) * QB)
+        out_ref[:, part] = (values_ref[:, part].astype(jnp.float32) * scales[:, j : j + 1]).astype(out_ref.dtype)
+
+
 def dequantize(values, scales):
-    height, breadth = values.shape
-    scaled = values.astype(jnp.float32).reshape(height, breadth // QB, QB) * scales[:, :, None]
-    return scaled.reshape(height, breadth).astype(jnp.bfloat16)
+    return pl.pallas_call(
+        dequantize_kernel,
+        out_shape=jax.ShapeDtypeStruct(values.shape, jnp.bfloat16),
+        cost_estimate=pl.CostEstimate(flops=values.size, bytes_accessed=4 * values.size, transcendentals=0),
+        name="dequantize",
+    )(values, scales.T)
 
 
 def shift(array, axis, size, by):
@@ -44,7 +54,7 @@
     ).astype(out_ref.dtype)
 
 
-def partial_product(gradients, weight, marks, tile=256):
+def partial_product(gradients, weight, marks, tile=512):
     tokens, hidden = gradients.shape
     width = weight.shape[0]
     return pl.pallas_call(

time: 229 us -> 228 us (level)
  the two profiles are of different devices: /device:TPU:10 before, /device:TPU:14 now
where the time goes in v3:
time: 228 us; the launch traced here: 227 us
  waiting for transfers between devices  138 us (61%)
  starting transfers between devices  45.2 us (20%)
  Pallas kernels  21.7 us (10%)
  between operations  14.2 us (6%)
  local copies, waits for them, and re-layouts  6.36 us (3%)
    ppermute x10, waiting for transfers between devices, shift(): lax.ppermute(array, axis, [(i, (i + by) % size) for i in range(size)])  91.4 us
    all_gather x1, waiting for transfers between devices, shards(): gradients = lax.all_gather(grad_local, ROW, axis=0, tiled=True)  46.3 us
    ppermute x10, starting transfers between devices, shift(): lax.ppermute(array, axis, [(i, (i + by) % size) for i in range(size)])  38.5 us
    pallas_call x1, Pallas kernels, outer_product(): pl.pallas_call(kernel, grid=(width // tile,), in_specs=[pl.BlockSpec(memo...  9.1 us
    pallas_call x1, Pallas kernels, partial_product(): pl.pallas_call(partial_kernel, grid=(tokens // tile,), in_specs=[pl.Block...  8.28 us
    all_to_all x1, starting transfers between devices, shards(): lax.all_to_all(over_z, 'yhi', 0, 0, tiled=True).reshape(NY, rows, -1)  6.6 us
    unnamed x23, local copies, waits for them, and re-layouts  5.65 us
  transfers between devices with their start and end apart: 13, of which 10 were waited for; matrix products, arithmetic and copies ran while one was open for 3% of the time, Pallas kernels for 5%

profile of v3, /device:TPU:14, one launch (start us, length us, event | category | flops | bytes accessed | tf_op | source)
XLA Modules:
  0.0 227.4 jit_solution(17343090029724655350)
XLA Ops:
  7.2 1.9 dequantize.2
  9.2 46.3 %all-gather.2.cloned.1.call-done.grad_ref.refs_1_ = bf16[2048,896]{1,0:T(8,128)(2,1)} async-done(((bf16[128,896]{1,0:T(8,128)(2,1)}), bf16[2048,896]{1,0:T(8,128)(2,1)}) %all-gather.2.cloned.1.call-update) | async-done | bytes 3670032 | tf_op jit(solution)/shard_map/all_gather | solution.py:147
  55.5 8.3 %partial_product.1 = bf16[2048,1024]{1,0:T(8,128)(2,1)} custom-call(bf16[2048,896]{1,0:T(8,128)(2,1)} %all-gather.2.cloned.1.call-done.grad_ref.refs_1_, bf16[1024,896]{1,0:T(8,128)(2,1)} %weight_ref.1), custom_call_target="tpu_custom_call" | custom-call | flops 3758096384 | bytes 9699328 | tf_op jit(solution)/shard_map/partial_product/pallas_call | solution.py:60
  63.8 1.8 dequantize.3
  65.6 7.0 %collective-permute-start = (bf16[64,1024]{1,0:T(8,128)(2,1)}, bf16[64,1024]{1,0:T(8,128)(2,1)S(1)}, u32[]{:S(2)}, u32[]{:S(2)}) collective-permute-start(bf16[64,1024]{1,0:T(8,128)(2,1)} %dequantize.3), channel_id=1, source_target_pairs={{0,2},{1,3},{2,0},{3,1},{4,6},{5,7},{6,4},{7,5},{8,10},{9,11},{10,... | collective-permute-start | bytes 393224 | tf_op jit(solution)/shard_map/ppermute | solution.py:33
  72.6 7.4 %collective-permute-done = bf16[64,1024]{1,0:T(8,128)(2,1)S(1)} collective-permute-done((bf16[64,1024]{1,0:T(8,128)(2,1)}, bf16[64,1024]{1,0:T(8,128)(2,1)S(1)}, u32[]{:S(2)}, u32[]{:S(2)}) %collective-permute-start) | collective-permute-done | bytes 131104 | tf_op jit(solution)/shard_map/ppermute | solution.py:33
  80.0 0.9 pad_maximum_fusion.refs_4_
  81.0 5.9 %collective-permute-start.2 = (bf16[128,1024]{1,0:T(8,128)(2,1)S(1)}, bf16[128,1024]{1,0:T(8,128)(2,1)S(1)}, u32[]{:S(2)}, u32[]{:S(2)}) collective-permute-start(bf16[128,1024]{1,0:T(8,128)(2,1)S(1)} %pad_maximum_fusion.refs_4_), channel_id=1, source_target_pairs={{0,28},{4,0},{8,4},{12,8},{16,12},{20,16},{24,20},{28,24},{1,29},{... | collective-permute-start | bytes 786440 | tf_op jit(solution)/shard_map/ppermute | solution.py:33
  86.8 1.9 collective-permute-start.1
  88.8 1.6 constant_dynamic-update-slice_fusion
  90.3 7.8 %collective-permute-done.2.refs_6_ = bf16[128,1024]{1,0:T(8,128)(2,1)S(1)} collective-permute-done((bf16[128,1024]{1,0:T(8,128)(2,1)S(1)}, bf16[128,1024]{1,0:T(8,128)(2,1)S(1)}, u32[]{:S(2)}, u32[]{:S(2)}) %collective-permute-start.2) | collective-permute-done | bytes 262176 | tf_op jit(solution)/shard_map/ppermute | solution.py:33
  98.1 5.6 %collective-permute-start.4 = (bf16[128,1024]{1,0:T(8,128)(2,1)S(1)}, bf16[128,1024]{1,0:T(8,128)(2,1)S(1)}, u32[]{:S(2)}, u32[]{:S(2)}) collective-permute-start(bf16[128,1024]{1,0:T(8,128)(2,1)S(1)} %collective-permute-done.2.refs_6_), channel_id=1, source_target_pairs={{0,28},{4,0},{8,4},{12,8},{16,12},{20,16},{24,20},{28,24},{1,29},{... | collective-permute-start | bytes 786440 | tf_op jit(solution)/shard_map/ppermute | solution.py:33
  104.2 1.9 collective-permute-start.3
  106.1 0.7 slice_dynamic-update-slice_fusion.6
  107.4 7.5 %collective-permute-done.4.refs_1_.refs_8_ = bf16[128,1024]{1,0:T(8,128)(2,1)S(1)} collective-permute-done((bf16[128,1024]{1,0:T(8,128)(2,1)S(1)}, bf16[128,1024]{1,0:T(8,128)(2,1)S(1)}, u32[]{:S(2)}, u32[]{:S(2)}) %collective-permute-start.4) | collective-permute-done | bytes 262176 | tf_op jit(solution)/shard_map/ppermute | solution.py:33
  114.9 5.6 %collective-permute-start.6 = (bf16[128,1024]{1,0:T(8,128)(2,1)S(1)}, bf16[128,1024]{1,0:T(8,128)(2,1)S(1)}, u32[]{:S(2)}, u32[]{:S(2)}) collective-permute-start(bf16[128,1024]{1,0:T(8,128)(2,1)S(1)} %collective-permute-done.4.refs_1_.refs_8_), channel_id=1, source_target_pairs={{0,28},{4,0},{8,4},{12,8},{16,12},{20,16},{24,20},{28,24},{1,29},{... | collective-permute-start | bytes 786440 | tf_op jit(solution)/shard_map/ppermute | solution.py:33
  120.5 0.8 collective-permute-done.3.refs_0_.refs_7_
  121.3 1.9 collective-permute-start.5
  123.2 0.7 slice_dynamic-update-slice_fusion.4
  124.5 13.7 %collective-permute-done.5.refs_9_ = bf16[128,1024]{1,0:T(8,128)(2,1)S(1)} collective-permute-done((bf16[128,1024]{1,0:T(8,128)(2,1)S(1)}, bf16[128,1024]{1,0:T(8,128)(2,1)S(1)}, u32[]{:S(2)}, u32[]{:S(2)}) %collective-permute-start.5) | collective-permute-done | bytes 262176 | tf_op jit(solution)/shard_map/ppermute | solution.py:33
  138.2 1.9 collective-permute-start.7
  140.1 0.7 slice_dynamic-update-slice_fusion.2
  140.8 0.7 slice_dynamic-update-slice_fusion.1
  141.5 6.2 %collective-permute-done.7.refs_11_ = bf16[128,1024]{1,0:T(8,128)(2,1)S(1)} collective-permute-done((bf16[128,1024]{1,0:T(8,128)(2,1)S(1)}, bf16[128,1024]{1,0:T(8,128)(2,1)S(1)}, u32[]{:S(2)}, u32[]{:S(2)}) %collective-permute-start.7) | collective-permute-done | bytes 262176 | tf_op jit(solution)/shard_map/ppermute | solution.py:33
  147.6 0.7 slice_dynamic-update-slice_fusion
  148.4 4.9 %collective-permute-start.9 = (bf16[512,1024]{1,0:T(8,128)(2,1)}, bf16[512,1024]{1,0:T(8,128)(2,1)}, u32[]{:S(2)}, u32[]{:S(2)}) collective-permute-start(bf16[512,1024]{1,0:T(8,128)(2,1)} %slice_dynamic-update-slice_fusion), channel_id=1, source_target_pairs={{0,3},{1,0},{2,1},{3,2},{4,7},{5,4},{6,5},{7,6},{8,11},{9,8},{10,9... | collective-permute-start | bytes 3145736 | tf_op jit(solution)/shard_map/ppermute | solution.py:33
  153.3 1.9 collective-permute-start.8
  155.2 6.6 %all-to-all-start = ((bf16[4,64,1024]{2,1,0:T(8,128)(2,1)}), bf16[4,64,1024]{2,1,0:T(8,128)(2,1)S(1)}, u32[]{:S(2)}, u32[]{:S(2)}) async-start(bf16[4,64,1024]{2,1,0:T(8,128)(2,1)} %bitcast.5), calls=%async_computation.1 | async-start | bytes 1048576 | tf_op jit(solution)/shard_map/all_to_all | solution.py:151
  163.0 31.1 %collective-permute-done.9.refs_3_ = bf16[512,1024]{1,0:T(8,128)(2,1)} collective-permute-done((bf16[512,1024]{1,0:T(8,128)(2,1)}, bf16[512,1024]{1,0:T(8,128)(2,1)}, u32[]{:S(2)}, u32[]{:S(2)}) %collective-permute-start.9) | collective-permute-done | bytes 1048608 | tf_op jit(solution)/shard_map/ppermute | solution.py:33
  194.1 16.6 %collective-permute-done.8.refs_2_ = bf16[512,1024]{1,0:T(8,128)(2,1)} collective-permute-done((bf16[512,1024]{1,0:T(8,128)(2,1)}, bf16[512,1024]{1,0:T(8,128)(2,1)}, u32[]{:S(2)}, u32[]{:S(2)}) %collective-permute-start.8) | collective-permute-done | bytes 1048608 | tf_op jit(solution)/shard_map/ppermute | solution.py:33
  210.7 9.1 %outer_product.1 = bf16[1024,896]{1,0:T(8,128)(2,1)} custom-call(s32[2]{0:T(128)} %pad_add_fusion.refs_0_, bf16[2048,896]{1,0:T(8,128)(2,1)} %all-gather.2.cloned.1.call-done.grad_ref.refs_1_, bf16[512,1024]{1,0:T(8,128)(2,1)} %collective-permute-done.8.refs_2_, bf16[512,1024]{1,0:T(8,128)(2,1)} %collective-permute-done.9.refs_3_, ...), custom_call_target="tpu_custom_call" | custom-call | flops 3758096384 | bytes 9699328 | tf_op jit(solution)/shard_map/outer_product/pallas_call | solution.py:100
  219.9 0.7 reduce_sum.12
  (28 shorter events, 3.1 us)
Async XLA Ops:
  7.2 48.3 %all-gather.2.cloned.1.call-start = ((), (), s32[]{:S(2)}) async-start(), calls=%async_computation.2 | async-start | bytes 3899392 | tf_op jit(solution)/shard_map/all_gather | solution.py:147
  9.2 146.0 %reduce-scatter.2.cloned.1.call-start = ((), (), s32[]{:S(2)}) async-start(), calls=%async_computation.3 | async-start | bytes 4718592 | tf_op jit(solution)/shard_map/reduce_scatter | solution.py:150
  65.6 14.4 %collective-permute-start = (bf16[64,1024]{1,0:T(8,128)(2,1)}, bf16[64,1024]{1,0:T(8,128)(2,1)S(1)}, u32[]{:S(2)}, u32[]{:S(2)}) collective-permute-start(bf16[64,1024]{1,0:T(8,128)(2,1)} %dequantize.3), channel_id=1, source_target_pairs={{0,2},{1,3},{2,0},{3,1},{4,6},{5,7},{6,4},{7,5},{8,10},{9,11},{10,... | collective-permute-start | bytes 393224 | tf_op jit(solution)/shard_map/ppermute | solution.py:33
  81.0 129.8 %copy-start.2 = (bf16[128,1024]{1,0:T(8,128)(2,1)}, bf16[128,1024]{1,0:T(8,128)(2,1)S(1)}, u32[]{:S(2)}) copy-start(bf16[128,1024]{1,0:T(8,128)(2,1)S(1)} %pad_maximum_fusion.refs_4_) | copy-start | bytes 786436
  81.0 17.1 %collective-permute-start.2 = (bf16[128,1024]{1,0:T(8,128)(2,1)S(1)}, bf16[128,1024]{1,0:T(8,128)(2,1)S(1)}, u32[]{:S(2)}, u32[]{:S(2)}) collective-permute-start(bf16[128,1024]{1,0:T(8,128)(2,1)S(1)} %pad_maximum_fusion.refs_4_), channel_id=1, source_target_pairs={{0,28},{4,0},{8,4},{12,8},{16,12},{20,16},{24,20},{28,24},{1,29},{... | collective-permute-start | bytes 786440 | tf_op jit(solution)/shard_map/ppermute | solution.py:33
  86.8 17.3 %collective-permute-start.1 = (bf16[128,1024]{1,0:T(8,128)(2,1)S(1)}, bf16[128,1024]{1,0:T(8,128)(2,1)S(1)}, u32[]{:S(2)}, u32[]{:S(2)}) collective-permute-start(bf16[128,1024]{1,0:T(8,128)(2,1)S(1)} %pad_maximum_fusion.refs_4_), channel_id=1, source_target_pairs={{0,4},{4,8},{8,12},{12,16},{16,20},{20,24},{24,28},{28,0},{1,5},{5... | collective-permute-start | bytes 786440 | tf_op jit(solution)/shard_map/ppermute | solution.py:33
  98.1 112.6 %copy-start.3 = (bf16[128,1024]{1,0:T(8,128)(2,1)}, bf16[128,1024]{1,0:T(8,128)(2,1)S(1)}, u32[]{:S(2)}) copy-start(bf16[128,1024]{1,0:T(8,128)(2,1)S(1)} %collective-permute-done.2.refs_6_) | copy-start | bytes 786436
  98.1 16.8 %collective-permute-start.4 = (bf16[128,1024]{1,0:T(8,128)(2,1)S(1)}, bf16[128,1024]{1,0:T(8,128)(2,1)S(1)}, u32[]{:S(2)}, u32[]{:S(2)}) collective-permute-start(bf16[128,1024]{1,0:T(8,128)(2,1)S(1)} %collective-permute-done.2.refs_6_), channel_id=1, source_target_pairs={{0,28},{4,0},{8,4},{12,8},{16,12},{20,16},{24,20},{28,24},{1,29},{... | collective-permute-start | bytes 786440 | tf_op jit(solution)/shard_map/ppermute | solution.py:33
  104.2 106.6 %copy-start.4 = (bf16[128,1024]{1,0:T(8,128)(2,1)}, bf16[128,1024]{1,0:T(8,128)(2,1)S(1)}, u32[]{:S(2)}) copy-start(bf16[128,1024]{1,0:T(8,128)(2,1)S(1)} %collective-permute-done.1.refs_5_) | copy-start | bytes 786436
  104.2 17.1 %collective-permute-start.3 = (bf16[128,1024]{1,0:T(8,128)(2,1)S(1)}, bf16[128,1024]{1,0:T(8,128)(2,1)S(1)}, u32[]{:S(2)}, u32[]{:S(2)}) collective-permute-start(bf16[128,1024]{1,0:T(8,128)(2,1)S(1)} %collective-permute-done.1.refs_5_), channel_id=1, source_target_pairs={{0,4},{4,8},{8,12},{12,16},{16,20},{20,24},{24,28},{28,0},{1,5},{5... | collective-permute-start | bytes 786440 | tf_op jit(solution)/shard_map/ppermute | solution.py:33
  114.9 47.5 %copy-start = (bf16[128,1024]{1,0:T(8,128)(2,1)}, bf16[128,1024]{1,0:T(8,128)(2,1)S(1)}, u32[]{:S(2)}) copy-start(bf16[128,1024]{1,0:T(8,128)(2,1)S(1)} %collective-permute-done.4.refs_1_.refs_8_) | copy-start | bytes 786436
  114.9 25.9 %collective-permute-start.6 = (bf16[128,1024]{1,0:T(8,128)(2,1)S(1)}, bf16[128,1024]{1,0:T(8,128)(2,1)S(1)}, u32[]{:S(2)}, u32[]{:S(2)}) collective-permute-start(bf16[128,1024]{1,0:T(8,128)(2,1)S(1)} %collective-permute-done.4.refs_1_.refs_8_), channel_id=1, source_target_pairs={{0,28},{4,0},{8,4},{12,8},{16,12},{20,16},{24,20},{28,24},{1,29},{... | collective-permute-start | bytes 786440 | tf_op jit(solution)/shard_map/ppermute | solution.py:33
  121.3 41.1 %copy-start.1 = (bf16[128,1024]{1,0:T(8,128)(2,1)}, bf16[128,1024]{1,0:T(8,128)(2,1)S(1)}, u32[]{:S(2)}) copy-start(bf16[128,1024]{1,0:T(8,128)(2,1)S(1)} %collective-permute-done.3.refs_0_.refs_7_) | copy-start | bytes 786436
  121.3 16.9 %collective-permute-start.5 = (bf16[128,1024]{1,0:T(8,128)(2,1)S(1)}, bf16[128,1024]{1,0:T(8,128)(2,1)S(1)}, u32[]{:S(2)}, u32[]{:S(2)}) collective-permute-start(bf16[128,1024]{1,0:T(8,128)(2,1)S(1)} %collective-permute-done.3.refs_0_.refs_7_), channel_id=1, source_target_pairs={{0,4},{4,8},{8,12},{12,16},{16,20},{20,24},{24,28},{28,0},{1,5},{5... | collective-permute-start | bytes 786440 | tf_op jit(solution)/shard_map/ppermute | solution.py:33
  138.2 72.5 %copy-start.6 = (bf16[128,1024]{1,0:T(8,128)(2,1)}, bf16[128,1024]{1,0:T(8,128)(2,1)S(1)}, u32[]{:S(2)}) copy-start(bf16[128,1024]{1,0:T(8,128)(2,1)S(1)} %collective-permute-done.5.refs_9_) | copy-start | bytes 786436
  138.2 9.5 %collective-permute-start.7 = (bf16[128,1024]{1,0:T(8,128)(2,1)S(1)}, bf16[128,1024]{1,0:T(8,128)(2,1)S(1)}, u32[]{:S(2)}, u32[]{:S(2)}) collective-permute-start(bf16[128,1024]{1,0:T(8,128)(2,1)S(1)} %collective-permute-done.5.refs_9_), channel_id=1, source_target_pairs={{0,4},{4,8},{8,12},{12,16},{16,20},{20,24},{24,28},{28,0},{1,5},{5... | collective-permute-start | bytes 786440 | tf_op jit(solution)/shard_map/ppermute | solution.py:33
  140.8 70.0 %copy-start.5 = (bf16[128,1024]{1,0:T(8,128)(2,1)}, bf16[128,1024]{1,0:T(8,128)(2,1)S(1)}, u32[]{:S(2)}) copy-start(bf16[128,1024]{1,0:T(8,128)(2,1)S(1)} %collective-permute-done.6.refs_10_) | copy-start | bytes 786436
  147.6 63.1 %copy-start.7 = (bf16[128,1024]{1,0:T(8,128)(2,1)}, bf16[128,1024]{1,0:T(8,128)(2,1)S(1)}, u32[]{:S(2)}) copy-start(bf16[128,1024]{1,0:T(8,128)(2,1)S(1)} %collective-permute-done.7.refs_11_) | copy-start | bytes 786436
  148.4 45.7 %collective-permute-start.9 = (bf16[512,1024]{1,0:T(8,128)(2,1)}, bf16[512,1024]{1,0:T(8,128)(2,1)}, u32[]{:S(2)}, u32[]{:S(2)}) collective-permute-start(bf16[512,1024]{1,0:T(8,128)(2,1)} %slice_dynamic-update-slice_fusion), channel_id=1, source_target_pairs={{0,3},{1,0},{2,1},{3,2},{4,7},{5,4},{6,5},{7,6},{8,11},{9,8},{10,9... | collective-permute-start | bytes 3145736 | tf_op jit(solution)/shard_map/ppermute | solution.py:33
  153.3 57.4 %collective-permute-start.8 = (bf16[512,1024]{1,0:T(8,128)(2,1)}, bf16[512,1024]{1,0:T(8,128)(2,1)}, u32[]{:S(2)}, u32[]{:S(2)}) collective-permute-start(bf16[512,1024]{1,0:T(8,128)(2,1)} %slice_dynamic-update-slice_fusion), channel_id=1, source_target_pairs={{0,1},{1,2},{2,3},{3,0},{4,5},{5,6},{6,7},{7,4},{8,9},{9,10},{10,1... | collective-permute-start | bytes 3145736 | tf_op jit(solution)/shard_map/ppermute | solution.py:33
  155.2 64.6 %all-to-all-start = ((bf16[4,64,1024]{2,1,0:T(8,128)(2,1)}), bf16[4,64,1024]{2,1,0:T(8,128)(2,1)S(1)}, u32[]{:S(2)}, u32[]{:S(2)}) async-start(bf16[4,64,1024]{2,1,0:T(8,128)(2,1)} %bitcast.5), calls=%async_computation.1 | async-start | bytes 1048576 | tf_op jit(solution)/shard_map/all_to_all | solution.py:151
Sparse Core Ops, SparseCore 0:
  10.7 44.7 all-gather.1
  63.9 77.2 reduce-scatter.1
